TPU v7x, 32 devices: a whole 2x2x4 slice. The times are simulated.
32 devices in a mesh: dp: 4 (over z), row: 2 (over x), col: 4 (over y, core).
Axes of the slice: x: 2, y: 2, z: 4, core: 2. Of those that a mesh axis runs over, the one named last changes fastest.
Arguments:
- tokens: bfloat16 [768, 16384], P('row', ('dp', 'col')), may hold values from -6 to 6
- ln_gain: float32 [768], P('row'), may hold values from 0.5 to 1.5
- ln_bias: float32 [768], P('row'), may hold values from -0.3 to 0.3
- qkv_weight: bfloat16 [768, 3, 768], P('row', None, 'col'), may hold values from -0.21875 to 0.21875
- out_weight: bfloat16 [768, 768], P('col', 'row'), may hold values from -6 to 6
- up_weight: bfloat16 [768, 3072], P('row', 'col'), may hold values from -0.21875 to 0.21875
- down_weight: bfloat16 [768, 3072], P('row', 'col'), may hold values from -0.21875 to 0.21875
- mod_weight: bfloat16 [3, 768, 768], P(None, 'row'), may hold values from -0.109375 to 0.109375
- timestep: int32 [8], replicated, may hold values from 0 to 999
- block_size: int32 [8], replicated, may hold values from 32 to 256, as said below
- cotangent: bfloat16 [768, 16384], P('row', ('dp', 'col')), may hold values from -6 to 6
Outputs:
- output: bfloat16 [768, 16384], P('row', ('dp', 'col'))
- tokens_grad: float32 [768, 16384], P('row', ('dp', 'col'))
- ln_gain_grad: float32 [768], P('row')
- ln_bias_grad: float32 [768], P('row')
- qkv_grad: float32 [768, 3, 768], P('row', None, 'col')
- out_grad: float32 [768, 768], P('col', 'row')
- up_grad: float32 [768, 3072], P('row', 'col')
- down_grad: float32 [768, 3072], P('row', 'col')
- mod_grad: float32 [3, 768, 768], P(None, 'row')
Inputs may be any that keep to these rules, and one draw needn't show every extreme that they name: `block_size`: each entry is 256 halved zero to three times; some sequence has 256.
All inputs are finite; a program needn't handle non-finite values.
Results may differ from a plain program's by a relative error of at most 0.02.
Values may be sent and summed in bfloat16 or wider, within the bound.
No kernel may reach another device: no remote copies, remote signals or barrier semaphores. Data moves between devices by JAX's collectives and lax.ppermute only.
A program may use at most 256 MiB of HBM per device.

v0:
```python
from functools import partial
import math
import jax
import jax.numpy as jnp
from jax import lax
from jax.sharding import PartitionSpec as P

HEAD_DIM = 64
LENGTH = 2048
EPSILON = 1e-05
HIGH = lax.Precision.HIGHEST


def time_embed(steps_in, width_all):
    half_width = width_all // 2
    frequency = jnp.exp(-math.log(10000.0) * jnp.arange(half_width, dtype=jnp.float32) / half_width)
    angles = steps_in.astype(jnp.float32)[:, None] * frequency[None, :]
    return jnp.concatenate([jnp.sin(angles), jnp.cos(angles)], axis=1)


def rope_tables(length, head_width):
    half_dim = head_width // 2
    frequency = jnp.exp(-math.log(10000.0) * jnp.arange(half_dim, dtype=jnp.float32) / half_dim)
    angles = jnp.arange(length, dtype=jnp.float32)[:, None] * frequency[None, :]
    return (jnp.cos(angles), jnp.sin(angles))


def rotate(vector, cosine, sine_tab):
    half_dim = vector.shape[-1] // 2
    front_half, back_half = (vector[..., :half_dim], vector[..., half_dim:])
    return jnp.concatenate(
        [front_half * cosine - back_half * sine_tab, back_half * cosine + front_half * sine_tab],
        axis=-1,
    )


def unrotate(grads_in, cosine, sine_tab):
    half_dim = grads_in.shape[-1] // 2
    front_half, back_half = (grads_in[..., :half_dim], grads_in[..., half_dim:])
    return jnp.concatenate(
        [front_half * cosine + back_half * sine_tab, back_half * cosine - front_half * sine_tab],
        axis=-1,
    )


def token_totals(first_terms, second_terms):
    return lax.psum((jnp.sum(first_terms, axis=1), jnp.sum(second_terms, axis=1)), "row")


def norm_forward(values, width_all):
    sum_plain, sum_square = token_totals(values, values * values)
    mean_row = sum_plain / width_all
    inv_std = lax.rsqrt(sum_square / width_all - mean_row * mean_row + EPSILON)
    return ((values - mean_row[:, None]) * inv_std[:, None], inv_std)


def norm_backward(grad_norm, normed, inv_std, width_all):
    sum_plain, sum_cross = token_totals(grad_norm, grad_norm * normed)
    return inv_std[:, None] * (
        grad_norm - sum_plain[:, None] / width_all - normed * (sum_cross[:, None] / width_all)
    )


def gather_col(local_part):
    return lax.all_gather(local_part, "col", axis=0, tiled=True)


def gather_rows(local_part):
    return lax.all_gather(local_part, "row", axis=0, tiled=True)


def row_product(gathered, tile_part):
    return lax.psum_scatter(
        jnp.dot(gathered, tile_part, preferred_element_type=jnp.float32),
        "row",
        scatter_dimension=0,
        tiled=True,
    )


def col_product(gathered, tile_part):
    return lax.psum_scatter(
        jnp.dot(gathered, tile_part, preferred_element_type=jnp.float32),
        "col",
        scatter_dimension=0,
        tiled=True,
    )


def block_index(block_lens, length):
    positions = jnp.arange(length, dtype=jnp.int32)
    return positions[None, :] // block_lens[:, None]


def masked_scores(query_part, key_rows, key_block, query_block, score_scale):
    scores = (
        jnp.einsum("sqhd,skhd->shqk", query_part, key_rows, preferred_element_type=jnp.float32)
        * score_scale
    )
    visible = key_block[:, None, None, :] <= query_block[:, None, :, None]
    return jnp.where(visible, scores, -1e30)


def attend_forward(queries, key_rows, value_rows, block_lens):
    length = queries.shape[1]
    rows_per = min(512, length)
    score_scale = queries.shape[3] ** (-0.5)
    key_block = block_index(block_lens, length)

    def one_block(offset):
        query_part = lax.dynamic_slice_in_dim(queries, offset, rows_per, 1)
        query_block = lax.dynamic_slice_in_dim(key_block, offset, rows_per, 1)
        scores = masked_scores(query_part, key_rows, key_block, query_block, score_scale)
        row_top = jnp.max(scores, axis=-1, keepdims=True)
        raised = jnp.exp(scores - row_top)
        row_total = jnp.sum(raised, axis=-1, keepdims=True)
        weights = (raised / row_total).astype(jnp.bfloat16)
        block_out = jnp.einsum(
            "shqk,skhd->sqhd", weights, value_rows, preferred_element_type=jnp.float32
        )
        return (block_out, row_top[..., 0] + jnp.log(row_total[..., 0]))

    offsets = jnp.arange(0, length, rows_per, dtype=jnp.int32)
    block_outs, log_totals = lax.map(one_block, offsets)
    return (jnp.moveaxis(block_outs, 0, 1).reshape(queries.shape), log_totals)


def attend_backward(queries, key_rows, value_rows, grad_mixed, log_totals, block_lens):
    length = queries.shape[1]
    rows_per = min(512, length)
    score_scale = queries.shape[3] ** (-0.5)
    key_block = block_index(block_lens, length)

    def one_block(running, element):
        grad_keys, grad_values = running
        offset, log_part = element
        query_part = lax.dynamic_slice_in_dim(queries, offset, rows_per, 1)
        grad_part = lax.dynamic_slice_in_dim(grad_mixed, offset, rows_per, 1)
        query_block = lax.dynamic_slice_in_dim(key_block, offset, rows_per, 1)
        scores = masked_scores(query_part, key_rows, key_block, query_block, score_scale)
        weights = jnp.exp(scores - log_part[..., None])
        grad_weights = jnp.einsum(
            "sqhd,skhd->shqk", grad_part, value_rows, preferred_element_type=jnp.float32
        )
        grad_scores = weights * (
            grad_weights - jnp.sum(weights * grad_weights, axis=-1, keepdims=True)
        )
        grad_scores = grad_scores.astype(jnp.bfloat16)
        grad_query = (
            jnp.einsum("shqk,skhd->sqhd", grad_scores, key_rows, preferred_element_type=jnp.float32)
            * score_scale
        )
        grad_keys = (
            grad_keys
            + jnp.einsum(
                "shqk,sqhd->skhd", grad_scores, query_part, preferred_element_type=jnp.float32
            )
            * score_scale
        )
        grad_values = grad_values + jnp.einsum(
            "shqk,sqhd->skhd",
            weights.astype(jnp.bfloat16),
            grad_part,
            preferred_element_type=jnp.float32,
        )
        return ((grad_keys, grad_values), grad_query)

    offsets = jnp.arange(0, length, rows_per, dtype=jnp.int32)
    zero_grads = jnp.zeros(queries.shape, jnp.float32)
    (grad_keys, grad_values), grad_queries = lax.scan(
        one_block, (zero_grads, zero_grads), (offsets, log_totals)
    )
    return (jnp.moveaxis(grad_queries, 0, 1).reshape(queries.shape), grad_keys, grad_values)


def local(
    tokens,
    ln_gain,
    ln_bias,
    qkv_weight,
    out_weight,
    up_weight,
    down_weight,
    mod_weight,
    timestep,
    block_size,
    cotangent,
):
    n_row = lax.axis_size("row")
    n_col = lax.axis_size("col")
    width_all = mod_weight.shape[2]
    feat_local, local_tokens = tokens.shape
    group_tokens = local_tokens * n_col
    seq_here = group_tokens // n_row // LENGTH
    heads_here = qkv_weight.shape[2] // HEAD_DIM
    group_index = lax.axis_index("dp")
    first_token = group_index * group_tokens + lax.axis_index("col") * local_tokens
    seq_count = max(1, local_tokens // LENGTH)
    token_span = local_tokens // seq_count
    steps_here = lax.dynamic_slice_in_dim(timestep, first_token // LENGTH, seq_count, 0)
    embedded = time_embed(steps_here, width_all)
    modulation = jnp.einsum("nd,ked->kne", embedded, mod_weight.astype(jnp.float32), precision=HIGH)

    def per_token(table):
        return jnp.broadcast_to(table[:, None, :], (seq_count, token_span, feat_local)).reshape(
            local_tokens, feat_local
        )

    def per_sequence(values):
        return jnp.sum(values.reshape(seq_count, token_span, feat_local), axis=1)

    scale_tok = per_token(modulation[0])
    shift_tok = per_token(modulation[1])
    gate_tok = per_token(modulation[2])
    resid = tokens.astype(jnp.float32).T
    norm_one, inv_one = norm_forward(resid, width_all)
    act_one = (norm_one * ln_gain + ln_bias).astype(jnp.bfloat16)
    act_one_all = gather_col(act_one)
    qkv_tile = qkv_weight.reshape(feat_local, -1)
    projected = row_product(act_one_all, qkv_tile).reshape(
        seq_here, LENGTH, 3, heads_here, HEAD_DIM
    )
    cosine, sine_tab = rope_tables(LENGTH, HEAD_DIM)
    cosine = cosine[None, :, None, :]
    sine_tab = sine_tab[None, :, None, :]
    queries = rotate(projected[:, :, 0], cosine, sine_tab).astype(jnp.bfloat16)
    key_rows = rotate(projected[:, :, 1], cosine, sine_tab).astype(jnp.bfloat16)
    value_rows = projected[:, :, 2].astype(jnp.bfloat16)
    seq_first = (group_index * n_row + lax.axis_index("row")) * seq_here
    block_lens = lax.dynamic_slice_in_dim(block_size, seq_first, seq_here, 0)
    attended, log_totals = attend_forward(queries, key_rows, value_rows, block_lens)
    attn_mix = attended.reshape(seq_here * LENGTH, heads_here * HEAD_DIM).astype(jnp.bfloat16)
    attn_mix_all = gather_rows(attn_mix)
    branch_one = col_product(attn_mix_all, out_weight)
    hidden_one = resid + branch_one
    norm_two, inv_two = norm_forward(hidden_one, width_all)
    act_two = (norm_two * (1.0 + scale_tok) + shift_tok).astype(jnp.bfloat16)
    act_two_all = gather_col(act_two)
    pre_act = row_product(act_two_all, up_weight)
    gelu_out = jax.nn.gelu(pre_act, approximate=True).astype(jnp.bfloat16)
    gelu_all = gather_rows(gelu_out)
    branch_two = col_product(gelu_all, down_weight.T)
    result = hidden_one + (1.0 + gate_tok) * branch_two
    grad_out = cotangent.astype(jnp.float32).T
    gate_term = grad_out * branch_two
    grad_two = (grad_out * (1.0 + gate_tok)).astype(jnp.bfloat16)
    grad_two_all = gather_col(grad_two)
    grad_gelu = row_product(grad_two_all, down_weight)
    down_grad = jnp.einsum("td,tf->df", grad_two_all, gelu_all, preferred_element_type=jnp.float32)
    _, gelu_pull = jax.vjp(partial(jax.nn.gelu, approximate=True), pre_act)
    grad_pre = gelu_pull(grad_gelu)[0].astype(jnp.bfloat16)
    grad_pre_all = gather_rows(grad_pre)
    grad_act_two = col_product(grad_pre_all, up_weight.T)
    up_grad = jnp.einsum("td,tf->df", act_two_all, grad_pre_all, preferred_element_type=jnp.float32)
    scale_term = grad_act_two * norm_two
    grad_hidden = grad_out + norm_backward(
        grad_act_two * (1.0 + scale_tok), norm_two, inv_two, width_all
    )
    grad_one = grad_hidden.astype(jnp.bfloat16)
    grad_one_all = gather_col(grad_one)
    grad_attn = row_product(grad_one_all, out_weight.T)
    out_grad = jnp.einsum(
        "tc,td->cd", attn_mix_all, grad_one_all, preferred_element_type=jnp.float32
    )
    grad_attn = grad_attn.astype(jnp.bfloat16).reshape(seq_here, LENGTH, heads_here, HEAD_DIM)
    grad_queries, grad_keys, grad_values = attend_backward(
        queries, key_rows, value_rows, grad_attn, log_totals, block_lens
    )
    grad_queries = unrotate(grad_queries, cosine, sine_tab)
    grad_keys = unrotate(grad_keys, cosine, sine_tab)
    grad_projected = jnp.stack([grad_queries, grad_keys, grad_values], axis=2).astype(jnp.bfloat16)
    grad_projected = grad_projected.reshape(seq_here * LENGTH, 3 * heads_here * HEAD_DIM)
    grad_proj_all = gather_rows(grad_projected)
    grad_act_one = col_product(grad_proj_all, qkv_tile.T)
    qkv_grad = jnp.einsum(
        "td,tk->dk", act_one_all, grad_proj_all, preferred_element_type=jnp.float32
    ).reshape(qkv_weight.shape)
    gain_part = jnp.sum(grad_act_one * norm_one, axis=0)
    bias_part = jnp.sum(grad_act_one, axis=0)
    tokens_grad = grad_hidden + norm_backward(grad_act_one * ln_gain, norm_one, inv_one, width_all)
    grad_mod = jnp.stack(
        [per_sequence(scale_term), per_sequence(grad_act_two), per_sequence(gate_term)]
    )
    mod_part = jnp.einsum("nd,kne->ked", embedded, grad_mod, precision=HIGH)
    gain_grad, bias_grad, mod_grad = (
        lax.psum(gain_part.astype(jnp.bfloat16), ("dp", "col")).astype(jnp.float32),
        lax.psum(bias_part.astype(jnp.bfloat16), ("dp", "col")).astype(jnp.float32),
        lax.psum(mod_part.astype(jnp.bfloat16), ("dp", "col")).astype(jnp.float32),
    )
    qkv_grad, out_grad, up_grad, down_grad = (
        lax.psum(qkv_grad.astype(jnp.bfloat16), "dp").astype(jnp.float32),
        lax.psum(out_grad.astype(jnp.bfloat16), "dp").astype(jnp.float32),
        lax.psum(up_grad.astype(jnp.bfloat16), "dp").astype(jnp.float32),
        lax.psum(down_grad.astype(jnp.bfloat16), "dp").astype(jnp.float32),
    )
    return (
        result.astype(jnp.bfloat16).T,
        tokens_grad.T,
        gain_grad,
        bias_grad,
        qkv_grad,
        out_grad,
        up_grad,
        down_grad,
        mod_grad,
    )


def solution(mesh):
    placed = (
        P("row", ("dp", "col")),
        P("row"),
        P("row"),
        P("row", None, "col"),
        P("col", "row"),
        P("row", "col"),
        P("row", "col"),
        P(None, "row", None),
        P(),
        P(),
        P("row", ("dp", "col")),
    )
    return jax.shard_map(
        local,
        mesh=mesh,
        in_specs=placed,
        out_specs=(
            P("row", ("dp", "col")),
            P("row", ("dp", "col")),
            P("row"),
            P("row"),
            P("row", None, "col"),
            P("col", "row"),
            P("row", "col"),
            P("row", "col"),
            P(None, "row", None),
        ),
        check_vma=False,
    )
```

profile of v0, /device:TPU:0, one launch (start us, length us, event | category | flops | bytes accessed | tf_op | source)
XLA Modules:
  0.0 1632.1 jit_solution(8770067134209926731)
XLA Ops:
  17.3 30.4 %all-gather.9.cloned.1.call-done = bf16[4096,384]{1,0:T(8,128)(2,1)} async-done(((bf16[1024,384]{1,0:T(8,128)(2,1)}), bf16[4096,384]{1,0:T(8,128)(2,1)}) %all-gather.9.cloned.1.call-update) | async-done | bytes 3145744 | tf_op jit(solution)/shard_map/all_gather | solution.py:65
  47.7 7.0 fusion.85
  58.9 106.6 %reduce-scatter.9.cloned.1.call-done = f32[2048,576]{0,1:T(8,128)} async-done(((f32[4096,576]{0,1:T(8,128)}), f32[2048,576]{0,1:T(8,128)}) %reduce-scatter.9.cloned.1.call-update) | async-done | bytes 4718608 | tf_op jit(solution)/shard_map/reduce_scatter | solution.py:73
  170.5 98.7 %while.27 = (s32[]{:T(128)}, bf16[4,1,512,3,64]{2,4,3,1,0:T(8,128)(2,1)}, f32[4,1,3,512]{3,2,1,0:T(4,128)S(1)}, s32[1,2048]{1,0:T(1,128)S(1)}, s32[4]{0:T(128)S(...) while((s32[]{:T(128)}, ...), condition=%wide.region_8.10_spmd, body=%wide.region_5.9_spmd.sunk | while | flops 844102144 | bytes 50471144 | solution.py:124
  173.8 7.0 fusion.137
  180.8 6.8 fusion.138
  187.7 6.7 fusion.139
  198.5 7.0 fusion.137
  205.5 6.8 fusion.138
  212.3 6.7 fusion.139
  223.2 7.0 fusion.137
  230.2 6.8 fusion.138
  237.0 6.7 fusion.139
  247.9 7.0 fusion.137
  254.9 6.8 fusion.138
  261.7 6.7 fusion.139
  272.4 27.1 %all-gather.11.cloned.1.call-done = bf16[4096,192]{0,1:T(8,128)(2,1)} async-done(((bf16[2048,192]{0,1:T(8,128)(2,1)}), bf16[4096,192]{0,1:T(8,128)(2,1)}) %all-gather.11.cloned.1.call-update) | async-done | bytes 1572880 | tf_op jit(solution)/shard_map/all_gather | solution.py:69
  311.7 52.2 %reduce-scatter.11.cloned.1.call-done = f32[1024,384]{1,0:T(8,128)} async-done(((f32[4096,384]{1,0:T(8,128)}), f32[1024,384]{1,0:T(8,128)}) %reduce-scatter.11.cloned.1.call-update) | async-done | bytes 1572880 | tf_op jit(solution)/shard_map/reduce_scatter | solution.py:82
  374.6 19.8 %all-gather.17.cloned.1.call-done = bf16[4096,384]{1,0:T(8,128)(2,1)} async-done(((bf16[1024,384]{1,0:T(8,128)(2,1)}), bf16[4096,384]{1,0:T(8,128)(2,1)}) %all-gather.17.cloned.1.call-update) | async-done | bytes 3145744 | tf_op jit(solution)/shard_map/all_gather | solution.py:65
  394.4 10.4 fusion.89
  404.9 20.0 %all-gather.13.cloned.1.call-done = bf16[4096,384]{1,0:T(8,128)(2,1)} async-done(((bf16[1024,384]{1,0:T(8,128)(2,1)}), bf16[4096,384]{1,0:T(8,128)(2,1)}) %all-gather.13.cloned.1.call-update) | async-done | bytes 3145744 | tf_op jit(solution)/shard_map/all_gather | solution.py:65
  425.0 10.5 fusion.87
  436.0 135.8 %reduce-scatter.17.cloned.1.call-done = f32[2048,768]{1,0:T(8,128)} async-done(((f32[4096,768]{1,0:T(8,128)}), f32[2048,768]{1,0:T(8,128)}) %reduce-scatter.17.cloned.1.call-update) | async-done | bytes 6291472 | tf_op jit(solution)/shard_map/reduce_scatter | solution.py:73
  571.8 146.9 %reduce-scatter.13.cloned.1.call-done = f32[2048,768]{1,0:T(8,128)} async-done(((f32[4096,768]{1,0:T(8,128)}), f32[2048,768]{1,0:T(8,128)}) %reduce-scatter.13.cloned.1.call-update) | async-done | bytes 6291472 | tf_op jit(solution)/shard_map/reduce_scatter | solution.py:73
  718.7 9.0 fusion.51
  728.4 79.9 %all-gather.19.cloned.1.call-done = bf16[4096,768]{1,0:T(8,128)(2,1)} async-done(((bf16[2048,768]{1,0:T(8,128)(2,1)}), bf16[4096,768]{1,0:T(8,128)(2,1)}) %all-gather.19.cloned.1.call-update) | async-done | bytes 6291472 | tf_op jit(solution)/shard_map/all_gather | solution.py:69
  808.3 9.4 fusion.90
  817.7 72.3 %all-gather.15.cloned.1.call-done = bf16[4096,768]{1,0:T(8,128)(2,1)} async-done(((bf16[2048,768]{1,0:T(8,128)(2,1)}), bf16[4096,768]{1,0:T(8,128)(2,1)}) %all-gather.15.cloned.1.call-update) | async-done | bytes 6291472 | tf_op jit(solution)/shard_map/all_gather | solution.py:69
  890.0 9.4 fusion.88
  899.5 52.0 %reduce-scatter.19.cloned.1.call-done = f32[1024,384]{1,0:T(8,128)} async-done(((f32[4096,384]{1,0:T(8,128)}), f32[1024,384]{1,0:T(8,128)}) %reduce-scatter.19.cloned.1.call-update) | async-done | bytes 1572880 | tf_op jit(solution)/shard_map/reduce_scatter | solution.py:82
  959.2 53.5 %reduce-scatter.15.cloned.1.call-done = f32[1024,384]{1,0:T(8,128)} async-done(((f32[4096,384]{1,0:T(8,128)}), f32[1024,384]{1,0:T(8,128)}) %reduce-scatter.15.cloned.1.call-update) | async-done | bytes 1572880 | tf_op jit(solution)/shard_map/reduce_scatter | solution.py:82
  1017.0 28.6 %all-gather.21.cloned.1.call-done = bf16[4096,384]{1,0:T(8,128)(2,1)} async-done(((bf16[1024,384]{1,0:T(8,128)(2,1)}), bf16[4096,384]{1,0:T(8,128)(2,1)}) %all-gather.21.cloned.1.call-update) | async-done | bytes 3145744 | tf_op jit(solution)/shard_map/all_gather | solution.py:65
  1050.5 43.5 %reduce-scatter.21.cloned.1.call-done = f32[2048,192]{0,1:T(8,128)} async-done(((f32[4096,192]{0,1:T(8,128)}), f32[2048,192]{0,1:T(8,128)}) %reduce-scatter.21.cloned.1.call-update) | async-done | bytes 1572880 | tf_op jit(solution)/shard_map/reduce_scatter | solution.py:73
  1096.4 173.6 %while.28 = (s32[]{:T(128)}, f32[1,2048,3,64]{1,3,2,0:T(8,128)}, f32[1,2048,3,64]{1,3,2,0:T(8,128)}, f32[4,1,512,3,64]{2,0,4,3,1:T(4,128)}, s32[4]{0:T(128)S(1)}...) while((s32[]{:T(128)}, f32[1,2048,3,64]{1,3,2,0:T(8,128)}, ...), condition=%wide.region_25.27_spmd.clone, body=%wide.region_23.26_spmd.clone.sunk | while | flops 2063563264 | bytes 151970208 | solution.py:170
  1130.4 8.6 dynamic_update_slice.19
  1145.7 6.3 fusion.150
  1174.1 8.6 dynamic_update_slice.19
  1217.7 8.6 dynamic_update_slice.19
  1261.2 8.6 dynamic_update_slice.19
  1278.4 6.4 convolution_convert_fusion.1
  1284.8 7.1 convolution_convert_fusion
  1297.5 42.6 %all-gather.23.cloned.1.call-done = bf16[4096,576]{0,1:T(8,128)(2,1)} async-done(((bf16[2048,576]{0,1:T(8,128)(2,1)}), bf16[4096,576]{0,1:T(8,128)(2,1)}) %all-gather.23.cloned.1.call-update) | async-done | bytes 4718608 | tf_op jit(solution)/shard_map/all_gather | solution.py:69
  1340.1 6.7 convolution_convert_fusion.2
  1347.1 8.4 fusion.92
  1357.9 82.4 %all-reduce.9.cloned.1.call-done = bf16[3,384,768]{2,1,0:T(8,128)(2,1)} async-done(((bf16[3,384,768]{2,1,0:T(8,128)(2,1)}), bf16[3,384,768]{2,1,0:T(8,128)(2,1)}) %all-reduce.9.cloned.1.call-update) | async-done | bytes 1769488 | tf_op jit(solution)/shard_map/psum | solution.py:288
  1443.8 73.8 %all-reduce.11.cloned.1.call-done = (bf16[384,3,192]{0,2,1:T(8,128)(2,1)}, bf16[192,384]{1,0:T(8,128)(2,1)}, bf16[384,768]{1,0:T(8,128)(2,1)}, bf16[384,768]{1,0:T(8,128)(2,1)}) async-done(((bf16[384,3,192]{0,2,1:T(8,128)(2,1)}, bf16[192,384]{1,0:T(8,128)(2,1)}, bf16[384,768]{1,0:T(8,128)(2,1)}, bf16[384,768]{1,0:T(8,128)(2,1)}), (bf16[384,3,192]{0,2,1:T(8,128)(2,1)}, bf16[192,384]{1,0:T(8,128)(2,1)}, ...) | async-done | bytes 1769488 | tf_op jit(solution)/shard_map/psum | solution.py:291
  1524.6 53.3 %reduce-scatter.23.cloned.1.call-done = f32[1024,384]{1,0:T(8,128)} async-done(((f32[4096,384]{1,0:T(8,128)}), f32[1024,384]{1,0:T(8,128)}) %reduce-scatter.23.cloned.1.call-update) | async-done | bytes 1572880 | tf_op jit(solution)/shard_map/reduce_scatter | solution.py:82
  1580.2 32.1 %all-reduce.4 = (bf16[384]{0:T(512)(128)(2,1)S(1)}, bf16[384]{0:T(512)(128)(2,1)S(1)}) all-reduce(bf16[384]{0:T(512)(128)(2,1)S(1)} %get-tuple-element.173, bf16[384]{0:T(512)(128)(2,1)S(1)} %get-tuple-element.178), channel_id=1, replica_groups=mesh['dp'=4,'row'=2,'col'=4] {'dp','col'}, use_global_device_ids=true, to_apply=%region_32.34 | all-reduce | flops 768 | bytes 3072 | tf_op jit(solution)/shard_map/psum | solution.py:286
  (303 shorter events, 239.1 us)
Async XLA Ops:
  7.2 300.2 %copy-start = (bf16[3,384,768]{2,1,0:T(8,128)(2,1)S(1)}, bf16[3,384,768]{2,1,0:T(8,128)(2,1)}, u32[]{:S(2)}) copy-start(bf16[3,384,768]{2,1,0:T(8,128)(2,1)} %param.24) | copy-start | bytes 5308420
  7.2 8.7 copy-start.34
  7.2 8.7 copy-start.43
  7.2 40.5 %copy-start.28 = (bf16[384,3,192]{0,2,1:T(8,128)(2,1)S(1)}, bf16[384,3,192]{0,2,1:T(8,128)(2,1)}, u32[]{:S(2)}) copy-start(bf16[384,3,192]{0,2,1:T(8,128)(2,1)} %param.20) | copy-start | bytes 1327108
  7.2 40.4 %all-gather.9.cloned.1.call-start = ((), (), s32[]{:S(2)}) async-start(), calls=%async_computation.8 | async-start | bytes 3932160 | tf_op jit(solution)/shard_map/all_gather | solution.py:65
  8.9 45.7 %copy-start.9 = (bf16[384,1024]{0,1:T(8,128)(2,1)}, bf16[384,1024]{0,1:T(8,128)(2,1)S(1)}, u32[]{:S(2)}) copy-start(bf16[384,1024]{0,1:T(8,128)(2,1)S(1)} %copy.24) | copy-start | bytes 2359300
  17.2 148.2 %reduce-scatter.9.cloned.1.call-start = ((), (), s32[]{:S(2)}) async-start(), calls=%async_computation.9 | async-start | bytes 14155776 | tf_op jit(solution)/shard_map/reduce_scatter | solution.py:73
  54.7 244.8 %all-gather.11.cloned.1.call-start = ((), (), s32[]{:S(2)}) async-start(), calls=%async_computation.10 | async-start | bytes 2359296 | tf_op jit(solution)/shard_map/all_gather | solution.py:69
  58.9 110.2 %copy-start.18 = (f32[2048,32]{0,1:T(8,128)}, f32[2048,32]{0,1:T(8,128)S(1)}, u32[]{:S(2)}) copy-start(f32[2048,32]{0,1:T(8,128)S(1)} %get-tuple-element.267) | copy-start | bytes 786436
  58.9 110.2 %copy-start.20 = (f32[2048,32]{0,1:T(8,128)}, f32[2048,32]{0,1:T(8,128)S(1)}, u32[]{:S(2)}) copy-start(f32[2048,32]{0,1:T(8,128)S(1)} %get-tuple-element.268) | copy-start | bytes 786436
  269.3 30.2 %copy-start.27 = (bf16[192,384]{1,0:T(8,128)(2,1)S(1)}, bf16[192,384]{1,0:T(8,128)(2,1)}, u32[]{:S(2)}) copy-start(bf16[192,384]{1,0:T(8,128)(2,1)} %param.21) | copy-start | bytes 442372
  272.2 91.8 %reduce-scatter.11.cloned.1.call-start = ((), (), s32[]{:S(2)}) async-start(), calls=%async_computation.11 | async-start | bytes 7864320 | tf_op jit(solution)/shard_map/reduce_scatter | solution.py:82
  304.9 89.5 %all-gather.17.cloned.1.call-start = ((), (), s32[]{:S(2)}) async-start(), calls=%async_computation.16 | async-start | bytes 3932160 | tf_op jit(solution)/shard_map/all_gather | solution.py:65
  308.9 55.0 %copy-start.10 = (bf16[384,1024]{0,1:T(8,128)(2,1)S(1)}, bf16[384,1024]{0,1:T(8,128)(2,1)}, u32[]{:S(2)}) copy-start(bf16[384,1024]{0,1:T(8,128)(2,1)} %copy-done.9) | copy-start | bytes 2359300
  310.5 56.1 %copy-start.16 = (bf16[384,1024]{0,1:T(8,128)(2,1)}, bf16[384,1024]{0,1:T(8,128)(2,1)S(1)}, u32[]{:S(2)}) copy-start(bf16[384,1024]{0,1:T(8,128)(2,1)S(1)} %copy.26) | copy-start | bytes 2359300
  311.6 113.3 %all-gather.13.cloned.1.call-start = ((), (), s32[]{:S(2)}) async-start(), calls=%async_computation.12 | async-start | bytes 3932160 | tf_op jit(solution)/shard_map/all_gather | solution.py:65
  366.6 27.8 %copy-start.24 = (bf16[384,768]{1,0:T(8,128)(2,1)S(1)}, bf16[384,768]{1,0:T(8,128)(2,1)}, u32[]{:S(2)}) copy-start(bf16[384,768]{1,0:T(8,128)(2,1)} %param.23) | copy-start | bytes 1769476
  374.5 197.3 %reduce-scatter.17.cloned.1.call-start = ((), (), s32[]{:S(2)}) async-start(), calls=%async_computation.17 | async-start | bytes 18874368 | tf_op jit(solution)/shard_map/reduce_scatter | solution.py:73
  404.8 20.1 %copy-start.23 = (bf16[384,768]{1,0:T(8,128)(2,1)S(1)}, bf16[384,768]{1,0:T(8,128)(2,1)}, u32[]{:S(2)}) copy-start(bf16[384,768]{1,0:T(8,128)(2,1)} %param.22) | copy-start | bytes 1769476
  404.9 313.9 %reduce-scatter.13.cloned.1.call-start = ((), (), s32[]{:S(2)}) async-start(), calls=%async_computation.13 | async-start | bytes 18874368 | tf_op jit(solution)/shard_map/reduce_scatter | solution.py:73
  435.5 372.7 %all-gather.19.cloned.1.call-start = ((), (), s32[]{:S(2)}) async-start(), calls=%async_computation.18 | async-start | bytes 9437184 | tf_op jit(solution)/shard_map/all_gather | solution.py:69
  727.8 162.3 %all-gather.15.cloned.1.call-start = ((), (), s32[]{:S(2)}) async-start(), calls=%async_computation.14 | async-start | bytes 9437184 | tf_op jit(solution)/shard_map/all_gather | solution.py:69
  728.3 223.1 %reduce-scatter.19.cloned.1.call-start = ((), (), s32[]{:S(2)}) async-start(), calls=%async_computation.19 | async-start | bytes 7864320 | tf_op jit(solution)/shard_map/reduce_scatter | solution.py:82
  817.6 72.4 %copy-start.25 = (bf16[384,768]{1,0:T(8,128)(2,1)S(1)}, bf16[384,768]{1,0:T(8,128)(2,1)}, u32[]{:S(2)}) copy-start(bf16[384,768]{1,0:T(8,128)(2,1)} %param.23) | copy-start | bytes 1769476
  817.7 195.0 %reduce-scatter.15.cloned.1.call-start = ((), (), s32[]{:S(2)}) async-start(), calls=%async_computation.15 | async-start | bytes 7864320 | tf_op jit(solution)/shard_map/reduce_scatter | solution.py:82
  899.4 52.0 %copy-start.12 = (f32[1024,384]{1,0:T(8,128)S(1)}, f32[1024,384]{1,0:T(8,128)}, u32[]{:S(2)}) copy-start(f32[1024,384]{1,0:T(8,128)} %get-tuple-element.238) | copy-start | bytes 4718596
  899.4 146.2 %all-gather.21.cloned.1.call-start = ((), (), s32[]{:S(2)}) async-start(), calls=%async_computation.20 | async-start | bytes 3932160 | tf_op jit(solution)/shard_map/all_gather | solution.py:65
  1016.9 77.1 %reduce-scatter.21.cloned.1.call-start = ((), (), s32[]{:S(2)}) async-start(), calls=%async_computation.21 | async-start | bytes 4718592 | tf_op jit(solution)/shard_map/reduce_scatter | solution.py:73
  1050.4 289.7 %all-gather.23.cloned.1.call-start = ((), (), s32[]{:S(2)}) async-start(), calls=%async_computation.22 | async-start | bytes 7077888 | tf_op jit(solution)/shard_map/all_gather | solution.py:69
  1126.4 12.6 copy-start.5
  1126.4 12.6 copy-start.8
  1169.5 13.2 copy-start.5
  1169.5 13.2 copy-start.8
  1213.1 13.2 copy-start.5
  1213.1 13.2 copy-start.8
  1256.6 13.2 copy-start.5
  1256.6 13.2 copy-start.8
  1277.3 162.9 %all-reduce.9.cloned.1.call-start = ((), (), s32[]{:S(2)}) async-start(), calls=%async_computation.24 | async-start | bytes 3538944 | tf_op jit(solution)/shard_map/psum | solution.py:288
  1284.8 7.1 copy-start.42
  1284.8 7.1 copy-start.41
  1284.8 7.2 copy-start.40
  1293.5 224.1 %all-reduce.11.cloned.1.call-start = ((), (), s32[]{:S(2)}) async-start(), calls=%async_computation.25 | async-start | bytes 3538944 | tf_op jit(solution)/shard_map/psum | solution.py:291
  1297.5 49.7 %copy-start.29 = (bf16[384,3,192]{0,2,1:T(8,128)(2,1)S(1)}, bf16[384,3,192]{0,2,1:T(8,128)(2,1)}, u32[]{:S(2)}) copy-start(bf16[384,3,192]{0,2,1:T(8,128)(2,1)} %param.20) | copy-start | bytes 1327108
  1346.8 231.1 %reduce-scatter.23.cloned.1.call-start = ((), (), s32[]{:S(2)}) async-start(), calls=%async_computation.23 | async-start | bytes 7864320 | tf_op jit(solution)/shard_map/reduce_scatter | solution.py:82
  1443.8 134.1 %copy-start.11 = (bf16[384,1024]{0,1:T(8,128)(2,1)S(1)}, bf16[384,1024]{0,1:T(8,128)(2,1)}, u32[]{:S(2)}) copy-start(bf16[384,1024]{0,1:T(8,128)(2,1)} %copy-done.9) | copy-start | bytes 2359300
  1443.8 134.1 %copy-start.31 = (f32[1024]{0:T(1024)S(1)}, f32[1024]{0:T(1024)}, u32[]{:S(2)}) copy-start(f32[1024]{0:T(1024)} %copy-done.30) | copy-start | bytes 12292
  1443.8 134.1 %copy-start.33 = (f32[1024]{0:T(1024)S(1)}, f32[1024]{0:T(1024)}, u32[]{:S(2)}) copy-start(f32[1024]{0:T(1024)} %copy-done.32) | copy-start | bytes 12292
  1443.8 134.1 %copy-start.35 = (f32[384]{0:T(512)S(1)}, f32[384]{0:T(512)}, u32[]{:S(2)}) copy-start(f32[384]{0:T(512)} %param.18) | copy-start | bytes 4612
  (40 other events, 157.2 us)
Sparse Core Ops, SparseCore 0:
  17.3 30.2 all-gather.8
  54.8 110.6 reduce-scatter.8
  272.3 27.1 all-gather.10
  305.0 58.8 reduce-scatter.10
  365.9 28.4 all-gather.16
  396.4 28.4 all-gather.12
  427.3 144.5 reduce-scatter.16
  574.1 144.5 reduce-scatter.12
  727.9 80.3 all-gather.18
  809.6 80.3 all-gather.14
  892.6 58.8 reduce-scatter.18
  953.8 58.8 reduce-scatter.14
  1017.1 28.5 all-gather.20
  1050.6 43.3 reduce-scatter.20
  1277.4 62.6 all-gather.22
  1343.5 96.7 all-reduce.8
  1443.3 74.3 all-reduce.10
  1520.0 57.8 reduce-scatter.22
where the time goes:
time: 1640 us; the launch traced here: 1630 us
  waiting for transfers between devices  1120 us (68%)
  matrix products  243 us (15%)
  other arithmetic  111 us (7%)
  local copies, waits for them, and re-layouts  68.2 us (4%)
  blocking collectives  53.1 us (3%)
  between operations  16.6 us (1%)
  loops' own time  16.4 us (1%)
    reduce_scatter x4, waiting for transfers between devices, row_product(): lax.psum_scatter(jnp.dot(gathered, tile_part, preferred_element_type=jnp....  433 us
    all_gather x4, waiting for transfers between devices, gather_rows(): return lax.all_gather(local_part, 'row', axis=0, tiled=True)  222 us
    reduce_scatter x4, waiting for transfers between devices, col_product(): lax.psum_scatter(jnp.dot(gathered, tile_part, preferred_element_type=jnp....  211 us
    all_gather x4, waiting for transfers between devices, gather_col(): return lax.all_gather(local_part, 'col', axis=0, tiled=True)  98.9 us
    psum x1, waiting for transfers between devices, local(): lax.psum(mod_part.astype(jnp.bfloat16), ('dp', 'col')).astype(jnp.float32)  82.4 us
    psum x1, waiting for transfers between devices, local(): lax.psum(qkv_grad.astype(jnp.bfloat16), 'dp').astype(jnp.float32)  73.8 us
    dot_general x8, matrix products, masked_scores(): jnp.einsum('sqhd,skhd->shqk', query_part, key_rows, preferred_element_typ...  40.6 us
    dynamic_update_slice x8, local copies, waits for them, and re-layouts, attend_forward(): block_outs, log_totals = lax.map(one_block, offsets)  36.1 us
  transfers between devices with their start and end apart: 18, of which 18 were waited for; matrix products, arithmetic and copies ran while one was open for 6% of the time, Pallas kernels for 0%

commit v1 on v0

--- a/solution.py
+++ b/solution.py
@@ -11,6 +11,27 @@
 HIGH = lax.Precision.HIGHEST
 
 
+def joined_along(blocks, dim):
+    blocks = jnp.moveaxis(blocks, 0, dim)
+    shape = blocks.shape
+    return blocks.reshape(*shape[:dim], shape[dim] * shape[dim + 1], *shape[dim + 2 :])
+
+
+def collected_by_bits(x, axis):
+    size, index = (lax.axis_size(axis), lax.axis_index(axis))
+    blocks, distance = (x[None], 1)
+    while distance < size:
+        other = lax.ppermute(blocks, axis, [(i, i ^ distance) for i in range(size)])
+        low = index & distance == 0
+        blocks = jnp.concatenate([jnp.where(low, blocks, other), jnp.where(low, other, blocks)])
+        distance *= 2
+    return blocks
+
+
+def doubled_up(x, axis, dim):
+    return joined_along(collected_by_bits(x, axis), dim)
+
+
 def time_embed(steps_in, width_all):
     half_width = width_all // 2
     frequency = jnp.exp(-math.log(10000.0) * jnp.arange(half_width, dtype=jnp.float32) / half_width)
@@ -66,7 +87,7 @@
 
 
 def gather_rows(local_part):
-    return lax.all_gather(local_part, "row", axis=0, tiled=True)
+    return doubled_up(local_part, "row", 0)
 
 
 def row_product(gathered, tile_part):

time: 1640 us -> 1510 us (0.921)
  waiting for transfers between devices: 1120 us -> 991 us
  matrix products: 243 us -> 224 us
    all_gather x4 -> x0, waiting for transfers between devices: 222 us -> none  [gather_rows(): return lax.all_gather(local_part, 'row', axis=0, tiled=True)]
    ppermute x0 -> x4, waiting for transfers between devices: none -> 196 us  [collected_by_bits(): other = lax.ppermute(blocks, axis, [(i, i ^ distance) for i in range(size)])]
    reduce_scatter x4, waiting for transfers between devices: 211 us -> 155 us  [col_product(): lax.psum_scatter(jnp.dot(gathered, tile_part, preferred_element_type=jnp....]
    psum x1, waiting for transfers between devices: 82.4 us -> 33.5 us  [local(): lax.psum(mod_part.astype(jnp.bfloat16), ('dp', 'col')).astype(jnp.float32)]
  transfers between devices with their start and end apart: 18 -> 18, of which waited for: 18 -> 17; matrix products, arithmetic and copies ran while one was open for 6% -> 6% of each run, Pallas kernels for 0% -> 0%
where the time goes in v1:
time: 1510 us; the launch traced here: 1500 us
  waiting for transfers between devices  991 us (66%)
  matrix products  224 us (15%)
  other arithmetic  120 us (8%)
  local copies, waits for them, and re-layouts  80.8 us (5%)
  blocking collectives  53.1 us (4%)
  loops' own time  16.4 us (1%)
  between operations  16.2 us (1%)
    reduce_scatter x4, waiting for transfers between devices, row_product(): lax.psum_scatter(jnp.dot(gathered, tile_part, preferred_element_type=jnp....  433 us
    ppermute x4, waiting for transfers between devices, collected_by_bits(): other = lax.ppermute(blocks, axis, [(i, i ^ distance) for i in range(size)])  196 us
    reduce_scatter x4, waiting for transfers between devices, col_product(): lax.psum_scatter(jnp.dot(gathered, tile_part, preferred_element_type=jnp....  155 us
    all_gather x4, waiting for transfers between devices, gather_col(): return lax.all_gather(local_part, 'col', axis=0, tiled=True)  98.9 us
    psum x1, waiting for transfers between devices, local(): lax.psum(qkv_grad.astype(jnp.bfloat16), 'dp').astype(jnp.float32)  74 us
    dot_general x8, matrix products, masked_scores(): jnp.einsum('sqhd,skhd->shqk', query_part, key_rows, preferred_element_typ...  40.3 us
    dynamic_update_slice x8, local copies, waits for them, and re-layouts, attend_forward(): block_outs, log_totals = lax.map(one_block, offsets)  36.1 us
    psum x1, waiting for transfers between devices, local(): lax.psum(mod_part.astype(jnp.bfloat16), ('dp', 'col')).astype(jnp.float32)  33.5 us
  transfers between devices with their start and end apart: 18, of which 17 were waited for; matrix products, arithmetic and copies ran while one was open for 6% of the time, Pallas kernels for 0%

profile of v1, /device:TPU:0, one launch (start us, length us, event | category | flops | bytes accessed | tf_op | source)
XLA Modules:
  0.0 1504.6 jit_solution(12911043304762869255)
XLA Ops:
  17.3 30.4 %all-gather.5.cloned.1.call-done = bf16[4096,384]{1,0:T(8,128)(2,1)} async-done(((bf16[1024,384]{1,0:T(8,128)(2,1)}), bf16[4096,384]{1,0:T(8,128)(2,1)}) %all-gather.5.cloned.1.call-update) | async-done | bytes 3145744 | tf_op jit(solution)/shard_map/all_gather | solution.py:86
  47.7 7.0 fusion.92
  58.9 106.6 %reduce-scatter.9.cloned.1.call-done = f32[2048,576]{0,1:T(8,128)} async-done(((f32[4096,576]{0,1:T(8,128)}), f32[2048,576]{0,1:T(8,128)}) %reduce-scatter.9.cloned.1.call-update) | async-done | bytes 4718608 | tf_op jit(solution)/shard_map/reduce_scatter | solution.py:94
  170.6 98.4 %while.27 = (s32[]{:T(128)}, bf16[4,1,512,3,64]{2,4,3,1,0:T(8,128)(2,1)}, f32[4,1,3,512]{3,2,1,0:T(4,128)S(1)}, s32[1,2048]{1,0:T(1,128)S(1)}, s32[4]{0:T(128)S(...) while((s32[]{:T(128)}, ...), condition=%wide.region_8.10_spmd, body=%wide.region_5.9_spmd.sunk | while | flops 844102144 | bytes 50471144 | solution.py:145
  173.8 6.9 fusion.143
  180.7 6.8 fusion.144
  187.6 6.7 fusion.145
  198.4 6.9 fusion.143
  205.3 6.8 fusion.144
  212.2 6.7 fusion.145
  223.0 6.9 fusion.143
  230.0 6.8 fusion.144
  236.8 6.7 fusion.145
  247.6 6.9 fusion.143
  254.5 6.8 fusion.144
  261.4 6.7 fusion.145
  274.7 19.1 %collective-permute-done = bf16[1,2048,192]{1,2,0:T(8,128)(2,1)} collective-permute-done((bf16[1,2048,192]{1,2,0:T(8,128)(2,1)}, bf16[1,2048,192]{1,2,0:T(8,128)(2,1)}, u32[]{:S(2)}, u32[]{:S(2)}) %collective-permute-start) | collective-permute-done | bytes 786464 | tf_op jit(solution)/shard_map/ppermute | solution.py:24
  307.6 52.2 %reduce-scatter.11.cloned.1.call-done = f32[1024,384]{1,0:T(8,128)} async-done(((f32[4096,384]{1,0:T(8,128)}), f32[1024,384]{1,0:T(8,128)}) %reduce-scatter.11.cloned.1.call-update) | async-done | bytes 1572880 | tf_op jit(solution)/shard_map/reduce_scatter | solution.py:103
  370.4 19.9 %all-gather.9.cloned.1.call-done = bf16[4096,384]{1,0:T(8,128)(2,1)} async-done(((bf16[1024,384]{1,0:T(8,128)(2,1)}), bf16[4096,384]{1,0:T(8,128)(2,1)}) %all-gather.9.cloned.1.call-update) | async-done | bytes 3145744 | tf_op jit(solution)/shard_map/all_gather | solution.py:86
  390.3 10.4 fusion.96
  400.8 20.0 %all-gather.7.cloned.1.call-done = bf16[4096,384]{1,0:T(8,128)(2,1)} async-done(((bf16[1024,384]{1,0:T(8,128)(2,1)}), bf16[4096,384]{1,0:T(8,128)(2,1)}) %all-gather.7.cloned.1.call-update) | async-done | bytes 3145744 | tf_op jit(solution)/shard_map/all_gather | solution.py:86
  420.8 10.5 fusion.94
  431.8 135.7 %reduce-scatter.17.cloned.1.call-done = f32[2048,768]{1,0:T(8,128)} async-done(((f32[4096,768]{1,0:T(8,128)}), f32[2048,768]{1,0:T(8,128)}) %reduce-scatter.17.cloned.1.call-update) | async-done | bytes 6291472 | tf_op jit(solution)/shard_map/reduce_scatter | solution.py:94
  567.6 146.9 %reduce-scatter.13.cloned.1.call-done = f32[2048,768]{1,0:T(8,128)} async-done(((f32[4096,768]{1,0:T(8,128)}), f32[2048,768]{1,0:T(8,128)}) %reduce-scatter.13.cloned.1.call-update) | async-done | bytes 6291472 | tf_op jit(solution)/shard_map/reduce_scatter | solution.py:94
  714.4 8.5 fusion.55
  723.3 69.3 %collective-permute-done.2 = bf16[1,2048,768]{2,1,0:T(8,128)(2,1)S(1)} collective-permute-done((bf16[1,2048,768]{2,1,0:T(8,128)(2,1)S(1)}, bf16[1,2048,768]{2,1,0:T(8,128)(2,1)S(1)}, u32[]{:S(2)}, u32[]{:S(2)}) %collective-permute-start.2) | collective-permute-done | bytes 3145760 | tf_op jit(solution)/shard_map/ppermute | solution.py:24
  802.3 68.5 %collective-permute-done.1 = bf16[1,2048,768]{2,1,0:T(8,128)(2,1)S(1)} collective-permute-done((bf16[1,2048,768]{2,1,0:T(8,128)(2,1)}, bf16[1,2048,768]{2,1,0:T(8,128)(2,1)S(1)}, u32[]{:S(2)}, u32[]{:S(2)}) %collective-permute-start.1) | collective-permute-done | bytes 3145760 | tf_op jit(solution)/shard_map/ppermute | solution.py:24
  890.9 49.9 %reduce-scatter.15.cloned.1.call-done = f32[1024,384]{1,0:T(8,128)} async-done(((f32[4096,384]{1,0:T(8,128)}), f32[1024,384]{1,0:T(8,128)}) %reduce-scatter.15.cloned.1.call-update) | async-done | bytes 1572880 | tf_op jit(solution)/shard_map/reduce_scatter | solution.py:103
  945.2 28.6 %all-gather.11.cloned.1.call-done = bf16[4096,384]{1,0:T(8,128)(2,1)} async-done(((bf16[1024,384]{1,0:T(8,128)(2,1)}), bf16[4096,384]{1,0:T(8,128)(2,1)}) %all-gather.11.cloned.1.call-update) | async-done | bytes 3145744 | tf_op jit(solution)/shard_map/all_gather | solution.py:86
  978.7 43.5 %reduce-scatter.21.cloned.1.call-done = f32[2048,192]{0,1:T(8,128)} async-done(((f32[4096,192]{0,1:T(8,128)}), f32[2048,192]{0,1:T(8,128)}) %reduce-scatter.21.cloned.1.call-update) | async-done | bytes 1572880 | tf_op jit(solution)/shard_map/reduce_scatter | solution.py:94
  1024.6 173.9 %while.28 = (s32[]{:T(128)}, f32[1,2048,3,64]{1,3,2,0:T(8,128)}, f32[1,2048,3,64]{1,3,2,0:T(8,128)}, f32[4,1,512,3,64]{2,0,4,3,1:T(4,128)}, s32[4]{0:T(128)S(1)}...) while((s32[]{:T(128)}, f32[1,2048,3,64]{1,3,2,0:T(8,128)}, ...), condition=%wide.region_25.27_spmd.clone, body=%wide.region_23.26_spmd.clone.sunk | while | flops 2063563264 | bytes 151970208 | solution.py:191
  1043.3 6.2 multiply_convert_fusion.4
  1058.7 8.6 dynamic_update_slice.19
  1073.9 6.4 fusion.156
  1086.4 6.2 multiply_convert_fusion.4
  1102.4 8.6 dynamic_update_slice.19
  1117.6 6.4 fusion.156
  1130.2 6.2 multiply_convert_fusion.4
  1146.1 8.6 dynamic_update_slice.19
  1161.3 6.4 fusion.156
  1173.8 6.2 multiply_convert_fusion.4
  1189.7 8.6 dynamic_update_slice.19
  1219.9 39.2 %collective-permute-done.3 = bf16[1,2048,576]{1,2,0:T(8,128)(2,1)} collective-permute-done((bf16[1,2048,576]{1,2,0:T(8,128)(2,1)}, bf16[1,2048,576]{1,2,0:T(8,128)(2,1)}, u32[]{:S(2)}, u32[]{:S(2)}) %collective-permute-start.3) | collective-permute-done | bytes 2359328 | tf_op jit(solution)/shard_map/ppermute | solution.py:24
  1269.0 8.3 fusion.99
  1279.5 33.5 %all-reduce.9.cloned.1.call-done = bf16[3,384,768]{2,1,0:T(8,128)(2,1)} async-done(((bf16[3,384,768]{2,1,0:T(8,128)(2,1)}), bf16[3,384,768]{2,1,0:T(8,128)(2,1)}) %all-reduce.9.cloned.1.call-update) | async-done | bytes 1769488 | tf_op jit(solution)/shard_map/psum | solution.py:309
  1316.7 74.0 %all-reduce.11.cloned.1.call-done = (bf16[384,3,192]{0,2,1:T(8,128)(2,1)}, bf16[192,384]{1,0:T(8,128)(2,1)}, bf16[384,768]{1,0:T(8,128)(2,1)}, bf16[384,768]{1,0:T(8,128)(2,1)}) async-done(((bf16[384,3,192]{0,2,1:T(8,128)(2,1)}, bf16[192,384]{1,0:T(8,128)(2,1)}, bf16[384,768]{1,0:T(8,128)(2,1)}, bf16[384,768]{1,0:T(8,128)(2,1)}), (bf16[384,3,192]{0,2,1:T(8,128)(2,1)}, bf16[192,384]{1,0:T(8,128)(2,1)}, ...) | async-done | bytes 1769488 | tf_op jit(solution)/shard_map/psum | solution.py:312
  1397.6 53.3 %reduce-scatter.23.cloned.1.call-done = f32[1024,384]{1,0:T(8,128)} async-done(((f32[4096,384]{1,0:T(8,128)}), f32[1024,384]{1,0:T(8,128)}) %reduce-scatter.23.cloned.1.call-update) | async-done | bytes 1572880 | tf_op jit(solution)/shard_map/reduce_scatter | solution.py:103
  1453.2 32.1 %all-reduce.4 = (bf16[384]{0:T(512)(128)(2,1)S(1)}, bf16[384]{0:T(512)(128)(2,1)S(1)}) all-reduce(bf16[384]{0:T(512)(128)(2,1)S(1)} %get-tuple-element.182, bf16[384]{0:T(512)(128)(2,1)S(1)} %get-tuple-element.187), channel_id=1, replica_groups=mesh['dp'=4,'row'=2,'col'=4] {'dp','col'}, use_global_device_ids=true, to_apply=%region_32.34 | all-reduce | flops 768 | bytes 3072 | tf_op jit(solution)/shard_map/psum | solution.py:307
  (329 shorter events, 244.5 us)
Async XLA Ops:
  7.2 296.1 %copy-start = (bf16[3,384,768]{2,1,0:T(8,128)(2,1)S(1)}, bf16[3,384,768]{2,1,0:T(8,128)(2,1)}, u32[]{:S(2)}) copy-start(bf16[3,384,768]{2,1,0:T(8,128)(2,1)} %param.24) | copy-start | bytes 5308420
  7.2 8.7 copy-start.39
  7.2 8.7 copy-start.48
  7.2 40.5 %copy-start.33 = (bf16[384,3,192]{0,2,1:T(8,128)(2,1)S(1)}, bf16[384,3,192]{0,2,1:T(8,128)(2,1)}, u32[]{:S(2)}) copy-start(bf16[384,3,192]{0,2,1:T(8,128)(2,1)} %param.20) | copy-start | bytes 1327108
  7.2 40.4 %all-gather.5.cloned.1.call-start = ((), (), s32[]{:S(2)}) async-start(), calls=%async_computation.8 | async-start | bytes 3932160 | tf_op jit(solution)/shard_map/all_gather | solution.py:86
  8.9 45.7 %copy-start.11 = (bf16[384,1024]{0,1:T(8,128)(2,1)}, bf16[384,1024]{0,1:T(8,128)(2,1)S(1)}, u32[]{:S(2)}) copy-start(bf16[384,1024]{0,1:T(8,128)(2,1)S(1)} %copy.32) | copy-start | bytes 2359300
  17.2 148.3 %reduce-scatter.9.cloned.1.call-start = ((), (), s32[]{:S(2)}) async-start(), calls=%async_computation.9 | async-start | bytes 14155776 | tf_op jit(solution)/shard_map/reduce_scatter | solution.py:94
  54.7 305.1 %reduce-scatter.11.cloned.1.call-start = ((), (), s32[]{:S(2)}) async-start(), calls=%async_computation.10 | async-start | bytes 7864320 | tf_op jit(solution)/shard_map/reduce_scatter | solution.py:103
  58.9 110.2 %copy-start.23 = (f32[2048,32]{0,1:T(8,128)}, f32[2048,32]{0,1:T(8,128)S(1)}, u32[]{:S(2)}) copy-start(f32[2048,32]{0,1:T(8,128)S(1)} %get-tuple-element.284) | copy-start | bytes 786436
  58.9 110.2 %copy-start.25 = (f32[2048,32]{0,1:T(8,128)}, f32[2048,32]{0,1:T(8,128)S(1)}, u32[]{:S(2)}) copy-start(f32[2048,32]{0,1:T(8,128)S(1)} %get-tuple-element.285) | copy-start | bytes 786436
  180.7 6.8 copy-start.26
  205.3 6.8 copy-start.26
  229.9 6.8 copy-start.26
  254.5 6.8 copy-start.26
  274.4 19.4 %collective-permute-start = (bf16[1,2048,192]{1,2,0:T(8,128)(2,1)}, bf16[1,2048,192]{1,2,0:T(8,128)(2,1)}, u32[]{:S(2)}, u32[]{:S(2)}) collective-permute-start(bf16[1,2048,192]{1,2,0:T(8,128)(2,1)} %convert_element_type.146), channel_id=1, source_target_pairs={{0,4},{4,0},{1,5},{5,1},{2,6},{6,2},{3,7},{7,3},{8,12},{12,8},{9,1... | collective-permute-start | bytes 2359304 | tf_op jit(solution)/shard_map/ppermute | solution.py:24
  300.7 89.6 %all-gather.9.cloned.1.call-start = ((), (), s32[]{:S(2)}) async-start(), calls=%async_computation.14 | async-start | bytes 3932160 | tf_op jit(solution)/shard_map/all_gather | solution.py:86
  304.8 55.0 %copy-start.12 = (bf16[384,1024]{0,1:T(8,128)(2,1)S(1)}, bf16[384,1024]{0,1:T(8,128)(2,1)}, u32[]{:S(2)}) copy-start(bf16[384,1024]{0,1:T(8,128)(2,1)} %copy-done.11) | copy-start | bytes 2359300
  306.4 56.1 %copy-start.19 = (bf16[384,1024]{0,1:T(8,128)(2,1)}, bf16[384,1024]{0,1:T(8,128)(2,1)S(1)}, u32[]{:S(2)}) copy-start(bf16[384,1024]{0,1:T(8,128)(2,1)S(1)} %copy.35) | copy-start | bytes 2359300
  307.5 113.3 %all-gather.7.cloned.1.call-start = ((), (), s32[]{:S(2)}) async-start(), calls=%async_computation.11 | async-start | bytes 3932160 | tf_op jit(solution)/shard_map/all_gather | solution.py:86
  362.5 27.8 %copy-start.29 = (bf16[384,768]{1,0:T(8,128)(2,1)S(1)}, bf16[384,768]{1,0:T(8,128)(2,1)}, u32[]{:S(2)}) copy-start(bf16[384,768]{1,0:T(8,128)(2,1)} %param.23) | copy-start | bytes 1769476
  370.4 197.2 %reduce-scatter.17.cloned.1.call-start = ((), (), s32[]{:S(2)}) async-start(), calls=%async_computation.15 | async-start | bytes 18874368 | tf_op jit(solution)/shard_map/reduce_scatter | solution.py:94
  400.7 20.1 %copy-start.28 = (bf16[384,768]{1,0:T(8,128)(2,1)S(1)}, bf16[384,768]{1,0:T(8,128)(2,1)}, u32[]{:S(2)}) copy-start(bf16[384,768]{1,0:T(8,128)(2,1)} %param.22) | copy-start | bytes 1769476
  400.8 313.7 %reduce-scatter.13.cloned.1.call-start = ((), (), s32[]{:S(2)}) async-start(), calls=%async_computation.12 | async-start | bytes 18874368 | tf_op jit(solution)/shard_map/reduce_scatter | solution.py:94
  431.4 450.5 %reduce-scatter.19.cloned.1.call-start = ((), (), s32[]{:S(2)}) async-start(), calls=%async_computation.16 | async-start | bytes 7864320 | tf_op jit(solution)/shard_map/reduce_scatter | solution.py:103
  722.9 69.7 %collective-permute-start.2 = (bf16[1,2048,768]{2,1,0:T(8,128)(2,1)S(1)}, bf16[1,2048,768]{2,1,0:T(8,128)(2,1)S(1)}, u32[]{:S(2)}, u32[]{:S(2)}) collective-permute-start(bf16[1,2048,768]{2,1,0:T(8,128)(2,1)S(1)} %get-tuple-element.254), channel_id=1, source_target_pairs={{0,4},{4,0},{1,5},{5,1},{2,6},{6,2},{3,7},{7,3},{8,12},{12,8},{9,1... | collective-permute-start | bytes 9437192 | tf_op jit(solution)/shard_map/ppermute | solution.py:24
  801.7 139.2 %reduce-scatter.15.cloned.1.call-start = ((), (), s32[]{:S(2)}) async-start(), calls=%async_computation.13 | async-start | bytes 7864320 | tf_op jit(solution)/shard_map/reduce_scatter | solution.py:103
  801.7 69.1 %collective-permute-start.1 = (bf16[1,2048,768]{2,1,0:T(8,128)(2,1)}, bf16[1,2048,768]{2,1,0:T(8,128)(2,1)S(1)}, u32[]{:S(2)}, u32[]{:S(2)}) collective-permute-start(bf16[1,2048,768]{2,1,0:T(8,128)(2,1)} %get-tuple-element.255), channel_id=1, source_target_pairs={{0,4},{4,0},{1,5},{5,1},{2,6},{6,2},{3,7},{7,3},{8,12},{12,8},{9,1... | collective-permute-start | bytes 9437192 | tf_op jit(solution)/shard_map/ppermute | solution.py:24
  881.8 91.9 %all-gather.11.cloned.1.call-start = ((), (), s32[]{:S(2)}) async-start(), calls=%async_computation.17 | async-start | bytes 3932160 | tf_op jit(solution)/shard_map/all_gather | solution.py:86
  945.1 77.0 %reduce-scatter.21.cloned.1.call-start = ((), (), s32[]{:S(2)}) async-start(), calls=%async_computation.18 | async-start | bytes 4718592 | tf_op jit(solution)/shard_map/reduce_scatter | solution.py:94
  978.6 334.5 %all-reduce.9.cloned.1.call-start = ((), (), s32[]{:S(2)}) async-start(), calls=%async_computation.20 | async-start | bytes 3538944 | tf_op jit(solution)/shard_map/psum | solution.py:309
  1024.7 6.6 copy-start.4
  1024.7 6.6 copy-start.9
  1054.6 12.6 copy-start.5
  1054.6 12.6 copy-start.10
  1097.8 13.2 copy-start.5
  1097.8 13.2 copy-start.10
  1141.5 13.2 copy-start.5
  1141.5 13.2 copy-start.10
  1185.1 13.2 copy-start.5
  1185.1 13.2 copy-start.10
  1204.3 6.8 slice-start.2
  1206.0 53.1 %collective-permute-start.3 = (bf16[1,2048,576]{1,2,0:T(8,128)(2,1)}, bf16[1,2048,576]{1,2,0:T(8,128)(2,1)}, u32[]{:S(2)}, u32[]{:S(2)}) collective-permute-start(bf16[1,2048,576]{1,2,0:T(8,128)(2,1)} %bitcast.32), channel_id=1, source_target_pairs={{0,4},{4,0},{1,5},{5,1},{2,6},{6,2},{3,7},{7,3},{8,12},{12,8},{9,1... | collective-permute-start | bytes 7077896 | tf_op jit(solution)/shard_map/ppermute | solution.py:24
  1216.2 174.4 %all-reduce.11.cloned.1.call-start = ((), (), s32[]{:S(2)}) async-start(), calls=%async_computation.21 | async-start | bytes 3538944 | tf_op jit(solution)/shard_map/psum | solution.py:312
  1268.6 182.2 %reduce-scatter.23.cloned.1.call-start = ((), (), s32[]{:S(2)}) async-start(), calls=%async_computation.19 | async-start | bytes 7864320 | tf_op jit(solution)/shard_map/reduce_scatter | solution.py:103
  1316.6 134.3 %copy-start.13 = (bf16[384,1024]{0,1:T(8,128)(2,1)S(1)}, bf16[384,1024]{0,1:T(8,128)(2,1)}, u32[]{:S(2)}) copy-start(bf16[384,1024]{0,1:T(8,128)(2,1)} %copy-done.11) | copy-start | bytes 2359300
  1316.6 134.3 %copy-start.36 = (f32[1024]{0:T(1024)S(1)}, f32[1024]{0:T(1024)}, u32[]{:S(2)}) copy-start(f32[1024]{0:T(1024)} %copy-done.35) | copy-start | bytes 12292
  1316.6 134.3 %copy-start.38 = (f32[1024]{0:T(1024)S(1)}, f32[1024]{0:T(1024)}, u32[]{:S(2)}) copy-start(f32[1024]{0:T(1024)} %copy-done.37) | copy-start | bytes 12292
  1316.7 134.3 %copy-start.40 = (f32[384]{0:T(512)S(1)}, f32[384]{0:T(512)}, u32[]{:S(2)}) copy-start(f32[384]{0:T(512)} %param.18) | copy-start | bytes 4612
  (49 other events, 155.9 us)
Sparse Core Ops, SparseCore 0:
  17.3 30.2 all-gather.4
  54.8 110.6 reduce-scatter.8
  300.9 58.8 reduce-scatter.10
  361.8 28.4 all-gather.8
  392.3 28.4 all-gather.6
  423.0 144.5 reduce-scatter.16
  569.9 144.5 reduce-scatter.12
  801.8 58.8 reduce-scatter.18
  882.0 58.8 reduce-scatter.14
  945.2 28.4 all-gather.10
  978.7 43.3 reduce-scatter.20
  1216.4 96.6 all-reduce.8
  1316.3 74.2 all-reduce.10
  1393.0 57.8 reduce-scatter.22
